TPU v7x, 512 devices: a whole 4x8x8 slice. The times are simulated.
512 devices in a mesh: sec: 32 (over x, z), mpo: 16 (over y, core).
Axes of the slice: x: 4, y: 8, z: 8, core: 2. Of those that a mesh axis runs over, the one named last changes fastest.
Arguments:
- psi_blocks: bfloat16 [256, 256, 256], P('sec'), may hold values from -6 to 6
- left_env: bfloat16 [64, 256, 256], P('mpo'), may hold values from -0.375 to 0.375
- right_env: bfloat16 [64, 256, 256], P('mpo'), may hold values from -0.046875 to 0.046875
- dest_index: int32 [16, 32, 32, 1], P('mpo', 'sec'), may hold values from 0 to 31; in each aligned block of 32 rows (0 to 31, 32 to 63, ..., all dimensions but the last counted through in order) at most 2 rows name the same one
- dest_slot: int32 [16, 32, 32], P('mpo', 'sec'), may hold values from 0 to 7
Outputs:
- sigma_blocks: float32 [256, 256, 256], P('sec', 'mpo')
Inputs may be any that keep to these rules, and one draw needn't show every extreme that they name: `dest_index`: in the 32 pairs of one device (fixed j and i), at most 2 name the same index of sec, and some device has exactly 2 for one index.
All inputs are finite; a program needn't handle non-finite values.
Results may differ from a plain program's by a relative error of at most 0.0041.
Values may be sent and summed in bfloat16 or wider, within the bound.
No kernel may reach another device: no remote copies, remote signals or barrier semaphores. Data moves between devices by JAX's collectives and lax.ppermute only.
A program may use at most 128 MiB of HBM per device.

v0:
```python
import jax
import jax.numpy as jnp
from jax import lax
from jax.sharding import PartitionSpec as P


def on_device(psi_blocks, left_env, right_env, dest_index, dest_slot):
    sectors = psi_blocks.shape[0]
    width = psi_blocks.shape[1]
    shards = lax.axis_size("sec")
    lefts = lax.all_to_all(left_env, "mpo", split_axis=1, concat_axis=0, tiled=True)
    rights = lax.all_gather(right_env, "mpo", axis=0, tiled=True)
    target = dest_index[:, :, :, 0] * sectors + dest_slot
    targets = lax.all_gather(target[0], "mpo", axis=0, tiled=True).reshape(-1)
    half = jnp.einsum("wrb,sbc->wsrc", lefts, psi_blocks, preferred_element_type=jnp.float32)
    half = half.astype(jnp.bfloat16)
    full = jnp.einsum("wsrc,wcd->wsrd", half, rights, preferred_element_type=jnp.float32)
    full = full.astype(jnp.bfloat16)
    rows = full.shape[2]
    select = jnp.arange(shards * sectors, dtype=jnp.int32)[:, None] == targets[None, :]
    partial = jnp.dot(
        select.astype(jnp.bfloat16),
        full.reshape(-1, rows * width),
        preferred_element_type=jnp.float32,
    )
    partial = partial.reshape(shards * sectors, rows, width)
    return lax.psum_scatter(partial, "sec", scatter_dimension=0, tiled=True)


def solution(mesh):
    in_specs = (
        P("sec", None, None),
        P("mpo", None, None),
        P("mpo", None, None),
        P("mpo", "sec", None, None),
        P("mpo", "sec", None),
    )
    out_specs = P("sec", "mpo", None)
    return jax.shard_map(
        on_device, mesh=mesh, in_specs=in_specs, out_specs=out_specs, check_vma=False
    )
```

profile of v0, /device:TPU:16, one launch (start us, length us, event | category | flops | bytes accessed | tf_op | source)
XLA Modules:
  0.0 338.5 jit_solution(17519727256088023447)
XLA Ops:
  6.5 0.0 copy-start
  6.5 0.0 all-gather.3.cloned.1.call-start
  6.5 0.7 all-gather.3.cloned.1.call-update
  7.3 2.3 copy.13
  9.5 9.1 %all-to-all-start = ((bf16[4,256,256]{2,0,1:T(4,128)(2,1)}), bf16[4,256,256]{2,0,1:T(4,128)(2,1)S(1)}, u32[]{:S(2)}, u32[]{:S(2)}) async-start(bf16[4,256,256]{2,0,1:T(4,128)(2,1)} %copy.13), calls=%async_computation | async-start | bytes 1048576 | tf_op jit(solution)/shard_map/all_to_all | solution.py:11
  18.6 0.0 reduce-scatter.2.cloned.1.call-start
  18.7 0.7 bitcast_add_fusion
  19.4 24.9 %all-gather = s32[16,1,32]{2,1,0:T(1,128)S(1)} all-gather(s32[1,1,32]{2,1,0:T(1,128)S(1)} %bitcast_add_fusion), channel_id=2, replica_groups=mesh['sec'=32,'mpo'=16] {'mpo'}, dimensions={0}, use_global_device_ids=true | all-gather | bytes 2176 | tf_op jit(solution)/shard_map/all_gather | solution.py:14
  44.2 0.5 broadcast.13
  44.7 0.7 reduce.3
  45.4 0.1 eq.16
  45.5 0.0 all-to-all-done
  45.5 0.1 copy.14
  45.6 28.0 %all-gather.3.cloned.1.call-done = bf16[64,256,256]{2,1,0:T(8,128)(2,1)} async-done(((bf16[4,256,256]{2,1,0:T(8,128)(2,1)}), bf16[64,256,256]{2,1,0:T(8,128)(2,1)}) %all-gather.3.cloned.1.call-update) | async-done | bytes 8388624 | tf_op jit(solution)/shard_map/all_gather | solution.py:12
  73.6 0.0 copy-done
  73.6 7.7 %convert_bitcast_fusion = bf16[64,8,16,256]{3,2,1,0:T(8,128)(2,1)} fusion(bf16[64,256,256]{2,1,0:T(8,128)(2,1)} %all-gather.3.cloned.1.call-done, bf16[64,16,256,1]{2,1,3,0:T(8,128)(2,1)S(1)} %bitcast.40, bf16[8,256,256]{2,1,0:T(8,128)(2,1)S(1)} %copy-done), kind=kOutput, calls=%fused_computation.3 | convolution fusion | flops 2151677952 | bytes 14155776 | tf_op jit(solution)/shard_map/wsrc,wcd->wsrd/dot_general | solution.py:17
  81.3 6.3 %copy.20 = bf16[64,8,16,256]{3,1,2,0:T(8,128)(2,1)} copy(bf16[64,8,16,256]{3,2,1,0:T(8,128)(2,1)} %convert_bitcast_fusion) | data formatting | bytes 8388608
  87.7 6.5 %copy.16 = bf16[4096,512]{1,0:T(8,128)(2,1)} copy(bf16[4096,512]{0,1:T(8,128)(2,1)} %bitcast.39) | data formatting | bytes 8388608 | tf_op jit(solution)/shard_map/dot_general | solution.py:21
  94.2 5.4 %fusion.13 = f32[256,16,256]{2,0,1:T(8,128)} fusion(bf16[16,256,512]{2,1,0:T(8,128)(2,1)} %bitcast.38, s32[512]{0:T(512)S(1)} %eq.16), kind=kOutput, calls=%fused_computation.9 | convolution fusion | flops 1073872896 | bytes 8390656 | tf_op jit(solution)/shard_map/dot_general | solution.py:21
  99.6 0.0 reduce-scatter.2.cloned.1.call-update
  99.6 230.4 %reduce-scatter.2.cloned.1.call-done = f32[8,16,256]{2,0,1:T(8,128)} async-done(((f32[256,16,256]{2,0,1:T(8,128)}), f32[8,16,256]{2,0,1:T(8,128)}) %reduce-scatter.2.cloned.1.call-update) | async-done | bytes 131088 | tf_op jit(solution)/shard_map/reduce_scatter | solution.py:27
  330.1 1.6 copy.17
  (1 shorter events, 0.0 us)
Async XLA Ops:
  6.5 67.1 %copy-start = (bf16[8,256,256]{2,1,0:T(8,128)(2,1)S(1)}, bf16[8,256,256]{2,1,0:T(8,128)(2,1)}, u32[]{:S(2)}) copy-start(bf16[8,256,256]{2,1,0:T(8,128)(2,1)} %param.5) | copy-start | bytes 3145732
  6.5 67.1 %all-gather.3.cloned.1.call-start = ((), (), s32[]{:S(2)}) async-start(), calls=%async_computation.2 | async-start | bytes 8912896 | tf_op jit(solution)/shard_map/all_gather | solution.py:12
  9.5 35.9 %all-to-all-start = ((bf16[4,256,256]{2,0,1:T(4,128)(2,1)}), bf16[4,256,256]{2,0,1:T(4,128)(2,1)S(1)}, u32[]{:S(2)}, u32[]{:S(2)}) async-start(bf16[4,256,256]{2,0,1:T(4,128)(2,1)} %copy.13), calls=%async_computation | async-start | bytes 1048576 | tf_op jit(solution)/shard_map/all_to_all | solution.py:11
  18.6 311.4 %reduce-scatter.2.cloned.1.call-start = ((), (), s32[]{:S(2)}) async-start(), calls=%async_computation.3 | async-start | bytes 4325376 | tf_op jit(solution)/shard_map/reduce_scatter | solution.py:27
Sparse Core Ops, SparseCore 0:
  9.5 64.1 all-gather.2
  99.7 230.2 reduce-scatter.1
where the time goes:
time: 339 us
  waiting for transfers between devices  259 us (76%)
  blocking collectives  24.9 us (7%)
  local copies, waits for them, and re-layouts  17.4 us (5%)
  between operations  13.4 us (4%)
  matrix products  13.1 us (4%)
  starting transfers between devices  9.13 us (3%)
    reduce_scatter x1, waiting for transfers between devices, on_device(): return lax.psum_scatter(partial, 'sec', scatter_dimension=0, tiled=True)  230 us
    all_gather x1, waiting for transfers between devices, on_device(): rights = lax.all_gather(right_env, 'mpo', axis=0, tiled=True)  28 us
    all_gather x1, blocking collectives, on_device(): targets = lax.all_gather(target[0], 'mpo', axis=0, tiled=True).reshape(-1)  24.9 us
    all_to_all x1, starting transfers between devices, on_device(): lax.all_to_all(left_env, 'mpo', split_axis=1, concat_axis=0, tiled=True)  9.09 us
    unnamed x4, local copies, waits for them, and re-layouts  8.62 us
    dot_general x1, matrix products, on_device(): jnp.einsum('wsrc,wcd->wsrd', half, rights, preferred_element_type=jnp.flo...  7.7 us
  transfers between devices with their start and end apart: 3, of which 2 were waited for; matrix products, arithmetic and copies ran while one was open for 1% of the time, Pallas kernels for 0%

commit v1 on v0

--- a/solution.py
+++ b/solution.py
@@ -9,7 +9,9 @@
     width = psi_blocks.shape[1]
     shards = lax.axis_size("sec")
     lefts = lax.all_to_all(left_env, "mpo", split_axis=1, concat_axis=0, tiled=True)
-    rights = lax.all_gather(right_env, "mpo", axis=0, tiled=True)
+    rights = jnp.concatenate(
+        lax.all_to_all(jnp.stack([right_env for _ in range(lax.axis_size("mpo"))]), "mpo", 0, 0), 0
+    )
     target = dest_index[:, :, :, 0] * sectors + dest_slot
     targets = lax.all_gather(target[0], "mpo", axis=0, tiled=True).reshape(-1)
     half = jnp.einsum("wrb,sbc->wsrc", lefts, psi_blocks, preferred_element_type=jnp.float32)

time: 339 us -> 503 us (1.48)
  the two profiles are of different devices: /device:TPU:16 before, /device:TPU:8 now
where the time goes in v1:
time: 503 us
  waiting for transfers between devices  231 us (46%)
  blocking collectives  216 us (43%)
  local copies, waits for them, and re-layouts  22 us (4%)
  between operations  13.5 us (3%)
  matrix products  13.1 us (3%)
  starting transfers between devices  6.43 us (1%)
    reduce_scatter x1, waiting for transfers between devices, on_device(): return lax.psum_scatter(partial, 'sec', scatter_dimension=0, tiled=True)  231 us
    all_gather x1, blocking collectives, on_device(): targets = lax.all_gather(target[0], 'mpo', axis=0, tiled=True).reshape(-1)  193 us
    all_to_all x1, blocking collectives, on_device(): lax.all_to_all(left_env, 'mpo', split_axis=1, concat_axis=0, tiled=True)  22.6 us
  transfers between devices with their start and end apart: 2, of which 1 were waited for; matrix products, arithmetic and copies ran while one was open for 0% of the time, Pallas kernels for 0%

profile of v1, /device:TPU:8, one launch (start us, length us, event | category | flops | bytes accessed | tf_op | source)
XLA Modules:
  0.0 502.7 jit_solution(14457508075850010995)
XLA Ops:
  6.5 0.0 copy-start
  6.5 1.5 copy.13
  8.1 22.6 %all_to_all.23 = bf16[4,256,256]{2,0,1:T(4,128)(2,1)S(1)} all-to-all(bf16[4,256,256]{2,0,1:T(4,128)(2,1)S(1)} %copy.13), channel_id=1, replica_groups=mesh['sec'=32,'mpo'=16] {'mpo'}, dimensions={1} | all-to-all | bytes 1048576 | tf_op jit(solution)/shard_map/all_to_all | solution.py:11
  30.7 5.3 %stack.2 = bf16[16,4,256,256]{3,2,1,0:T(8,128)(2,1)} broadcast(bf16[4,256,256]{2,1,0:T(8,128)(2,1)} %param.7), dimensions={1,2,3} | broadcast | bytes 8912896 | tf_op jit(solution)/shard_map/stack | solution.py:13
  36.0 0.0 copy-start.1
  36.0 0.0 copy-start.2
  36.0 6.4 %all-to-all-start.1 = ((bf16[16,4,256,256]{3,2,1,0:T(8,128)(2,1)}), bf16[16,4,256,256]{3,2,1,0:T(8,128)(2,1)}, u32[]{:S(2)}, u32[]{:S(2)}) async-start(bf16[16,4,256,256]{3,2,1,0:T(8,128)(2,1)} %stack.2), calls=%async_computation.1 | async-start | bytes 16777216 | tf_op jit(solution)/shard_map/all_to_all | solution.py:13
  42.4 0.0 reduce-scatter.2.cloned.1.call-start
  42.4 0.0 copy-done.1
  42.4 0.0 copy-done.2
  42.5 192.9 %all-gather = s32[16,1,32]{2,1,0:T(1,128)S(1)} all-gather(s32[1,1,32]{2,1,0:T(1,128)S(1)} %bitcast_add_fusion), channel_id=2, replica_groups=mesh['sec'=32,'mpo'=16] {'mpo'}, dimensions={0}, use_global_device_ids=true | all-gather | bytes 2176 | tf_op jit(solution)/shard_map/all_gather | solution.py:16
  235.4 0.5 broadcast.15
  235.9 0.7 reduce.3
  236.6 0.1 eq.16
  236.7 0.1 copy.14
  236.8 0.0 all-to-all-done.1
  236.8 0.0 copy-done
  236.8 7.7 %convert_bitcast_fusion = bf16[64,8,16,256]{3,2,1,0:T(8,128)(2,1)} fusion(bf16[64,256,256,1]{2,1,3,0:T(8,128)(2,1)} %bitcast.11, bf16[64,16,256,1]{2,1,3,0:T(8,128)(2,1)S(1)} %bitcast.39, bf16[8,256,256]{2,1,0:T(8,128)(2,1)S(1)} %copy-done), kind=kOutput, calls=%fused_computation.2 | convolution fusion | flops 2151677952 | bytes 14155776 | tf_op jit(solution)/shard_map/wsrc,wcd->wsrd/dot_general | solution.py:19
  244.5 6.3 %copy.20 = bf16[64,8,16,256]{3,1,2,0:T(8,128)(2,1)} copy(bf16[64,8,16,256]{3,2,1,0:T(8,128)(2,1)} %convert_bitcast_fusion) | data formatting | bytes 8388608
  250.8 6.5 %copy.16 = bf16[4096,512]{1,0:T(8,128)(2,1)} copy(bf16[4096,512]{0,1:T(8,128)(2,1)} %bitcast.38) | data formatting | bytes 8388608 | tf_op jit(solution)/shard_map/dot_general | solution.py:23
  257.4 5.4 %fusion.10 = f32[256,16,256]{2,0,1:T(8,128)} fusion(bf16[16,256,512]{2,1,0:T(8,128)(2,1)} %bitcast.37, s32[512]{0:T(512)S(1)} %eq.16), kind=kOutput, calls=%fused_computation.8 | convolution fusion | flops 1073872896 | bytes 8390656 | tf_op jit(solution)/shard_map/dot_general | solution.py:23
  262.8 0.0 reduce-scatter.2.cloned.1.call-update
  262.8 231.5 %reduce-scatter.2.cloned.1.call-done = f32[8,16,256]{2,0,1:T(8,128)} async-done(((f32[256,16,256]{2,0,1:T(8,128)}), f32[8,16,256]{2,0,1:T(8,128)}) %reduce-scatter.2.cloned.1.call-update) | async-done | bytes 131088 | tf_op jit(solution)/shard_map/reduce_scatter | solution.py:29
  494.3 1.6 copy.17
  (2 shorter events, 0.0 us)
Async XLA Ops:
  6.5 230.3 %copy-start = (bf16[8,256,256]{2,1,0:T(8,128)(2,1)S(1)}, bf16[8,256,256]{2,1,0:T(8,128)(2,1)}, u32[]{:S(2)}) copy-start(bf16[8,256,256]{2,1,0:T(8,128)(2,1)} %param.5) | copy-start | bytes 3145732
  36.0 6.4 %copy-start.1 = (s32[1,1,32]{2,1,0:T(1,128)S(1)}, s32[1,1,32]{2,1,0:T(1,128)}, u32[]{:S(2)}) copy-start(s32[1,1,32]{2,1,0:T(1,128)} %param.9) | copy-start | bytes 388
  36.0 6.5 %copy-start.2 = (s32[1,1,32,1]{2,3,1,0:T(1,128)S(1)}, s32[1,1,32,1]{2,3,1,0:T(1,128)}, u32[]{:S(2)}) copy-start(s32[1,1,32,1]{2,3,1,0:T(1,128)} %param.8) | copy-start | bytes 388
  36.0 200.8 %all-to-all-start.1 = ((bf16[16,4,256,256]{3,2,1,0:T(8,128)(2,1)}), bf16[16,4,256,256]{3,2,1,0:T(8,128)(2,1)}, u32[]{:S(2)}, u32[]{:S(2)}) async-start(bf16[16,4,256,256]{3,2,1,0:T(8,128)(2,1)} %stack.2), calls=%async_computation.1 | async-start | bytes 16777216 | tf_op jit(solution)/shard_map/all_to_all | solution.py:13
  42.4 451.9 %reduce-scatter.2.cloned.1.call-start = ((), (), s32[]{:S(2)}) async-start(), calls=%async_computation.3 | async-start | bytes 4325376 | tf_op jit(solution)/shard_map/reduce_scatter | solution.py:29
Sparse Core Ops, SparseCore 0:
  262.9 231.3 reduce-scatter.1
